TPU v7x, 128 devices: a whole 4x4x4 slice. The times are simulated.
128 devices in a mesh: ctx: 8 (over x, core), tp: 16 (over z, y).
Axes of the slice: x: 4, y: 4, z: 4, core: 2. Of those that a mesh axis runs over, the one named last changes fastest.
Arguments:
- out_grad: bfloat16 [8192, 4096], P('ctx', 'tp'), may hold values from -6 to 6
- pre_act: bfloat16 [8192, 4096], P('ctx', 'tp'), may hold values from -6 to 6
- normed: bfloat16 [8192, 12800], P('ctx', 'tp'), may hold values from -5 to 5
- inverse_std: float32 [8192], P('ctx'), may hold values from 0.5 to 2
- w_up: bfloat16 [4096, 12800], P(None, 'tp')
- w_down: bfloat16 [4096, 4096], P(None, 'tp'), may hold values from -0.09375 to 0.09375
- ln_gain: float32 [12800], P('tp'), may hold values from 0.25 to 1.75
- owner_map: int32 [8, 4], P('ctx'), may hold values from 0 to 15, as said below
Outputs:
- grad_w2: float32 [4096, 4096], P('ctx', 'tp')
- grad_w1: float32 [4096, 12800], P('ctx', 'tp')
- grad_b1: float32 [4096], P('tp')
- grad_b2: float32 [4096], P('tp')
- ln_grads: float32 [2, 12800], P(None, 'tp')
- vit_grad: bfloat16 [32768, 12800], P(('ctx', 'tp'))
Inputs may be any that keep to these rules, and one draw needn't show every extreme that they name: `owner_map`: within each context shard, every encoder rank owns at most 1 of the 4 images, and some rank owns exactly 1.
All inputs are finite; a program needn't handle non-finite values.
Results may differ from a plain program's by a relative error of at most 0.007.
Values may be sent and summed in bfloat16 or wider, within the bound.
A program may use at most 192 MiB of HBM per device.

v0:
```python
import math
import jax
import jax.numpy as jnp
from jax import lax
from jax.sharding import PartitionSpec as P


def gelu_parts(linear):
    normal_cdf = 0.5 * (1.0 + jax.scipy.special.erf(linear * 2.0 ** (-0.5)))
    density = jnp.exp(-0.5 * linear * linear) * (2.0 * math.pi) ** (-0.5)
    return (linear * normal_cdf, normal_cdf + linear * density)


def slot_numbers(owners, capacity):
    position = jnp.arange(owners.shape[0])
    earlier = (owners[None, :] == owners[:, None]) & (position[None, :] < position[:, None])
    return owners * capacity + jnp.sum(earlier.astype(jnp.int32), axis=1)


def row_product(left, right):
    return lax.dot_general(
        left, right, (((0,), (0,)), ((), ())), preferred_element_type=jnp.float32
    )


def per_device(out_grad, pre_act, normed, inverse_std, w_up, w_down, ln_gain, owner_map):
    ctx_count = lax.axis_size("ctx")
    tp_count = lax.axis_size("tp")
    row_count = out_grad.shape[0]
    grad_scale = float(row_count * ctx_count) ** (-0.5)
    gelu_value, gelu_slope = gelu_parts(pre_act.astype(jnp.float32))
    hidden = gelu_value.astype(jnp.bfloat16)
    full_grad = lax.all_gather(out_grad, "tp", axis=1, tiled=True)
    back_hidden = jnp.dot(full_grad, w_down, preferred_element_type=jnp.float32)
    back_part = (back_hidden * gelu_slope).astype(jnp.bfloat16)
    columns = full_grad
    grad_w2 = (
        lax.psum_scatter(row_product(columns, hidden), "ctx", scatter_dimension=0, tiled=True)
        * grad_scale
    )
    bias_down, bias_up = lax.psum(
        (
            jnp.sum(out_grad.astype(jnp.float32), axis=0),
            jnp.sum(back_part.astype(jnp.float32), axis=0),
        ),
        "ctx",
    )
    back_linear = lax.all_gather(back_part, "tp", axis=1, tiled=True)
    columns = back_linear
    grad_w1 = (
        lax.psum_scatter(row_product(columns, normed), "ctx", scatter_dimension=0, tiled=True)
        * grad_scale
    )
    norm_grad = jnp.dot(back_linear, w_up, preferred_element_type=jnp.float32)
    features = normed.astype(jnp.float32)
    gained = ln_gain[None, :] * norm_grad
    sum_first, sum_second = lax.psum(
        (jnp.sum(gained, axis=-1), jnp.sum(gained * features, axis=-1)), "tp"
    )
    full_width = float(normed.shape[1] * tp_count)
    mean_first = sum_first / full_width
    mean_second = sum_second / full_width
    visual = (
        inverse_std[:, None] * (gained - mean_first[:, None] - features * mean_second[:, None])
    ).astype(jnp.bfloat16)
    gain_sum, bias_sum = lax.psum(
        (jnp.sum(norm_grad * features, axis=0), jnp.sum(norm_grad, axis=0)), "ctx"
    )
    ln_grads = jnp.stack([gain_sum, bias_sum]) * grad_scale
    owners = owner_map[0]
    image_count = owners.shape[0]
    image_rows = row_count // image_count
    capacity = max(1, 2 * image_count // tp_count)
    slot_of = slot_numbers(owners, capacity)
    slot_ids = jnp.arange(tp_count * capacity)
    matches = slot_of[None, :] == slot_ids[:, None]
    present = jnp.any(matches, axis=1)
    source_image = jnp.sum(jnp.where(matches, jnp.arange(image_count)[None, :], 0), axis=1)
    images = visual.reshape(image_count, image_rows, visual.shape[1])
    picked = jnp.take(images, source_image, axis=0)
    outgoing = jnp.where(present[:, None, None], picked, jnp.zeros((), jnp.bfloat16)).reshape(
        tp_count * capacity * image_rows, visual.shape[1]
    )
    vit_grad = lax.all_to_all(outgoing, "tp", split_axis=0, concat_axis=1, tiled=True)
    return (grad_w2, grad_w1, bias_up * grad_scale, bias_down * grad_scale, ln_grads, vit_grad)


def solution(mesh):
    return jax.shard_map(
        per_device,
        mesh=mesh,
        in_specs=(
            P("ctx", "tp"),
            P("ctx", "tp"),
            P("ctx", "tp"),
            P("ctx"),
            P(None, "tp"),
            P(None, "tp"),
            P("tp"),
            P("ctx", None),
        ),
        out_specs=(
            P("ctx", "tp"),
            P("ctx", "tp"),
            P("tp"),
            P("tp"),
            P(None, "tp"),
            P(("ctx", "tp"), None),
        ),
        check_vma=False,
    )
```

profile of v0, /device:TPU:6, one launch (start us, length us, event | category | flops | bytes accessed | tf_op | source)
XLA Modules:
  0.0 356.5 jit_solution(15268767459479100883)
XLA Ops:
  7.2 0.0 all-gather.3.cloned.1.call-start
  7.2 0.7 all-gather.3.cloned.1.call-update
  7.9 0.0 all-gather.5.cloned.1.call-start
  8.0 83.0 %all-gather.3.cloned.1.call-done = bf16[1024,4096]{1,0:T(8,128)(2,1)} async-done(((bf16[1024,256]{1,0:T(8,128)(2,1)}), bf16[1024,4096]{1,0:T(8,128)(2,1)}) %all-gather.3.cloned.1.call-update) | async-done | bytes 8388624 | tf_op jit(solution)/shard_map/all_gather | solution.py:33
  91.0 6.8 %convert_reduce_fusion.1 = (f32[256]{0:T(256)S(1)}, bf16[1024,256]{1,0:T(8,128)(2,1)}) fusion(bf16[1024,256]{1,0:T(8,128)(2,1)} %param.9, bf16[1024,4096]{1,0:T(8,128)(2,1)} %all-gather.3.cloned.1.call-done, bf16[4096,256]{1,0:T(8,128)(2,1)S(1)} %copy-done), kind=kOutput, calls=%fused_computation.28 | convolution fusion | flops 2150891264 | bytes 11535360 | tf_op jit(solution)/shard_map/dot_general | solution.py:34
  97.8 0.0 all-gather.5.cloned.1.call-update
  97.8 0.0 reduce-scatter.3.cloned.1.call-start
  97.9 7.8 %convolution_bitcast_fusion = f32[4096,256]{0,1:T(8,128)} fusion(bf16[1024,4096]{1,0:T(8,128)(2,1)} %all-gather.3.cloned.1.call-done, bf16[1024,256]{1,0:T(8,128)(2,1)S(1)} %copy-done.4), kind=kOutput, calls=%fused_computation.2 | convolution fusion | flops 2149056512 | bytes 13107200 | tf_op jit(solution)/shard_map/dot_general | solution.py:21
  105.7 0.0 reduce-scatter.5.cloned.1.call-start
  105.8 69.9 %all-gather.5.cloned.1.call-done = bf16[1024,4096]{1,0:T(8,128)(2,1)} async-done(((bf16[1024,256]{1,0:T(8,128)(2,1)}), bf16[1024,4096]{1,0:T(8,128)(2,1)}) %all-gather.5.cloned.1.call-update) | async-done | bytes 8388624 | tf_op jit(solution)/shard_map/all_gather | solution.py:48
  175.7 13.2 %fusion.19 = f32[4096,800]{0,1:T(8,128)} fusion(bf16[1024,800]{0,1:T(8,128)(2,1)S(1)} %copy-done.3, bf16[1024,4096]{1,0:T(8,128)(2,1)} %all-gather.5.cloned.1.call-done), kind=kOutput, calls=%fused_computation.49 | convolution fusion | flops 6710886400 | bytes 23134208 | tf_op jit(solution)/shard_map/dot_general | solution.py:21
  188.9 0.6 copy-done.7
  189.5 0.2 convert_reduce_fusion.2
  189.7 0.1 select_reduce_fusion
  189.8 0.1 fusion.14
  190.0 13.3 %fusion.1 = (f32[1024]{0:T(1024)S(1)}, f32[800]{0:T(1024)S(1)}, f32[1024]{0:T(1024)S(1)}, f32[800]{0:T(1024)S(1)}, f32[1024,800]{0,1:T(8,128)}) fusion(bf16[1024,800]{0,1:T(8,128)(2,1)S(1)} %copy-done.3, f32[800]{0:T(1024)S(1)} %copy-done.5, bf16[1024,4096]{1,0:T(8,128)(2,1)} %all-gather.5.cloned.1.call-done, bf16[4096,800]{0,1:T(8,128)(2,1)} %param.12), kind=kOutput, calls=%fused_computation.7 | convolution fusion | flops 6717435904 | bytes 19875200 | tf_op jit(solution)/shard_map/dot_general | solution.py:54
  203.2 38.8 %all-reduce = (f32[1024]{0:T(1024)S(1)}, f32[1024]{0:T(1024)S(1)}) all-reduce(f32[1024]{0:T(1024)S(1)} %get-tuple-element.24, f32[1024]{0:T(1024)S(1)} %get-tuple-element.26), channel_id=1, replica_groups=mesh['ctx'=8,'tp'=16] {'tp'}, use_global_device_ids=true, to_apply=%region_16.17 | all-reduce | flops 2048 | bytes 16384 | tf_op jit(solution)/shard_map/psum | solution.py:57
  242.1 2.7 fusion.4
  244.8 0.1 copy.24
  244.9 3.8 %gather_fusion = bf16[16,256,800]{1,2,0:T(8,128)(2,1)} fusion(bf16[4,256,800]{1,2,0:T(8,128)(2,1)S(1)} %bitcast.27, s32[1024]{0:T(1024)S(1)} %pad_clamp_fusion), kind=kCustom, calls=%fused_computation | custom fusion | bytes 13107264 | tf_op jit(solution)/shard_map/jit(_take)/gather | solution.py:80
  248.7 6.6 %select_select_fusion = bf16[16,256,800]{1,2,0:T(8,128)(2,1)} fusion(bf16[16,256,800]{1,2,0:T(8,128)(2,1)} %gather_fusion, pred[16]{0:T(512)(128)(4,1)S(1)} %compare_and_fusion, pred[16]{0:T(512)(128)(4,1)S(1)} %fusion.14), kind=kLoop, calls=%fused_computation.1 | loop fusion | flops 6553600 | bytes 13107232 | tf_op jit(solution)/shard_map/jit(_where)/select_n | solution.py:81
  255.2 4.8 %all-to-all-start = ((bf16[16,256,800]{1,2,0:T(8,128)(2,1)}), bf16[16,256,800]{1,2,0:T(8,128)(2,1)}, u32[]{:S(2)}, u32[]{:S(2)}) async-start(bf16[16,256,800]{1,2,0:T(8,128)(2,1)} %select_select_fusion), calls=%async_computation.2 | async-start | bytes 13107200 | tf_op jit(solution)/shard_map/all_to_all | solution.py:84
  260.1 0.2 convert_reduce_fusion
  260.2 0.0 reduce-scatter.3.cloned.1.call-done
  260.3 1.1 broadcast_multiply_fusion.1
  261.4 1.0 copy.20
  262.4 12.1 %all-reduce.1 = (f32[256]{0:T(256)S(1)}, f32[256]{0:T(256)S(1)}, f32[1,800]{1,0:T(1,128)S(1)}, f32[1,800]{1,0:T(1,128)S(1)}) all-reduce(f32[256]{0:T(256)S(1)} %get-tuple-element.34, f32[256]{0:T(256)S(1)} %convert_reduce_fusion, f32[1,800]{1,0:T(1,128)S(1)} %stack.10, f32[1,800]{1,0:T(1,128)S(1)} %stack.9), channel_id=1, replica_groups=mesh['ctx'=8,'tp'=16] {'ctx'}, use_global_device_ids=true, to_apply=%region_3.0 | all-reduce | flops 2112 | bytes 16896 | tf_op jit(solution)/shard_map/psum | solution.py:41
  274.5 0.6 maximum_multiply_fusion
  275.1 0.6 broadcast_multiply_fusion.4
  275.7 61.9 %all-to-all-done = bf16[16,256,800]{1,2,0:T(8,128)(2,1)} async-done(((bf16[16,256,800]{1,2,0:T(8,128)(2,1)}), bf16[16,256,800]{1,2,0:T(8,128)(2,1)}, u32[]{:S(2)}, u32[]{:S(2)}) %all-to-all-start) | async-done | bytes 6553632 | tf_op jit(solution)/shard_map/all_to_all | solution.py:84
  337.5 9.7 %copy.21 = bf16[256,12800]{1,0:T(8,128)(2,1)} copy(bf16[256,12800]{0,1:T(8,128)(2,1)} %bitcast.7) | data formatting | bytes 13107200
  347.2 2.8 broadcast_multiply_fusion
  (25 shorter events, 0.1 us)
Async XLA Ops:
  7.2 83.8 %copy-start = (bf16[4096,256]{1,0:T(8,128)(2,1)S(1)}, bf16[4096,256]{1,0:T(8,128)(2,1)}, u32[]{:S(2)}) copy-start(bf16[4096,256]{1,0:T(8,128)(2,1)} %param.13) | copy-start | bytes 6291460
  7.2 83.8 %all-gather.3.cloned.1.call-start = ((), (), s32[]{:S(2)}) async-start(), calls=%async_computation.3 | async-start | bytes 8912896 | tf_op jit(solution)/shard_map/all_gather | solution.py:33
  7.9 89.9 %copy-start.4 = (bf16[1024,256]{1,0:T(8,128)(2,1)S(1)}, bf16[1024,256]{1,0:T(8,128)(2,1)}, u32[]{:S(2)}) copy-start(bf16[1024,256]{1,0:T(8,128)(2,1)} %param.9) | copy-start | bytes 1572868
  7.9 167.8 %all-gather.5.cloned.1.call-start = ((), (), s32[]{:S(2)}) async-start(), calls=%async_computation.5 | async-start | bytes 8912896 | tf_op jit(solution)/shard_map/all_gather | solution.py:48
  97.8 162.5 %reduce-scatter.3.cloned.1.call-start = ((), (), s32[]{:S(2)}) async-start(), calls=%async_computation.4 | async-start | bytes 4718592 | tf_op jit(solution)/shard_map/reduce_scatter | solution.py:38
  105.7 70.0 %copy-start.3 = (bf16[1024,800]{0,1:T(8,128)(2,1)S(1)}, bf16[1024,800]{0,1:T(8,128)(2,1)}, u32[]{:S(2)}) copy-start(bf16[1024,800]{0,1:T(8,128)(2,1)} %param.10) | copy-start | bytes 4915204
  105.7 241.5 %reduce-scatter.5.cloned.1.call-start = ((), (), s32[]{:S(2)}) async-start(), calls=%async_computation.6 | async-start | bytes 14745600 | tf_op jit(solution)/shard_map/reduce_scatter | solution.py:51
  188.9 0.7 copy-start.7
  188.9 1.0 copy-start.5
  189.9 52.2 %copy-start.6 = (f32[1024]{0:T(1024)S(1)}, f32[1024]{0:T(1024)}, u32[]{:S(2)}) copy-start(f32[1024]{0:T(1024)} %param.11) | copy-start | bytes 12292
  255.2 4.8 %copy-start.2 = (bf16[1024,256]{1,0:T(8,128)(2,1)S(1)}, bf16[1024,256]{1,0:T(8,128)(2,1)}, u32[]{:S(2)}) copy-start(bf16[1024,256]{1,0:T(8,128)(2,1)} %param.8) | copy-start | bytes 1572868
  255.2 82.3 %all-to-all-start = ((bf16[16,256,800]{1,2,0:T(8,128)(2,1)}), bf16[16,256,800]{1,2,0:T(8,128)(2,1)}, u32[]{:S(2)}, u32[]{:S(2)}) async-start(bf16[16,256,800]{1,2,0:T(8,128)(2,1)} %select_select_fusion), calls=%async_computation.2 | async-start | bytes 13107200 | tf_op jit(solution)/shard_map/all_to_all | solution.py:84
  337.5 12.5 %copy-start.1 = (bf16[4096,256]{1,0:T(8,128)(2,1)S(1)}, bf16[4096,256]{1,0:T(8,128)(2,1)}, u32[]{:S(2)}) copy-start(bf16[4096,256]{1,0:T(8,128)(2,1)} %param.13) | copy-start | bytes 6291460
Sparse Core Ops, SparseCore 0:
  10.1 80.8 all-gather.2
  97.9 77.7 all-gather.4
  178.1 33.4 reduce-scatter.2
  213.9 76.0 reduce-scatter.4
where the time goes:
time: 357 us
  waiting for transfers between devices  216 us (61%)
  blocking collectives  51 us (14%)
  matrix products  41.1 us (12%)
  local copies, waits for them, and re-layouts  15.2 us (4%)
  other arithmetic  14.9 us (4%)
  between operations  13.9 us (4%)
  starting transfers between devices  4.98 us (1%)
    all_gather x1, waiting for transfers between devices, per_device(): full_grad = lax.all_gather(out_grad, 'tp', axis=1, tiled=True)  83 us
    all_gather x1, waiting for transfers between devices, per_device(): back_linear = lax.all_gather(back_part, 'tp', axis=1, tiled=True)  69.9 us
    all_to_all x1, waiting for transfers between devices, per_device(): lax.all_to_all(outgoing, 'tp', split_axis=0, concat_axis=1, tiled=True)  61.9 us
    psum x1, blocking collectives, per_device(): lax.psum((jnp.sum(gained, axis=-1), jnp.sum(gained * features, axis=-1)),...  38.8 us
    dot_general x2, matrix products, row_product(): lax.dot_general(left, right, (((0,), (0,)), ((), ())), preferred_element_...  21 us
    dot_general x1, matrix products, per_device(): norm_grad = jnp.dot(back_linear, w_up, preferred_element_type=jnp.float32)  13.3 us
    psum x1, blocking collectives, per_device(): lax.psum((jnp.sum(out_grad.astype(jnp.float32), axis=0), jnp.sum(back_par...  12.1 us
    unnamed x18, local copies, waits for them, and re-layouts  11.3 us
  transfers between devices with their start and end apart: 5, of which 3 were waited for; matrix products, arithmetic and copies ran while one was open for 17% of the time, Pallas kernels for 0%

commit v1 on v0

--- a/solution.py
+++ b/solution.py
@@ -24,6 +24,13 @@
 
 
 def per_device(out_grad, pre_act, normed, inverse_std, w_up, w_down, ln_gain, owner_map):
+
+    def match_scales_in(named_axis, piece_in):
+        w2 = jnp.stack([piece_in for _ in range(jax.lax.psum(1, axis_name=named_axis))], axis=0)
+        met_up = jax.lax.all_to_all(w2, axis_name=named_axis, split_axis=0, concat_axis=0)
+        w1 = jnp.concatenate(met_up, axis=1)
+        return w1
+
     ctx_count = lax.axis_size("ctx")
     tp_count = lax.axis_size("tp")
     row_count = out_grad.shape[0]
@@ -45,7 +52,7 @@
         ),
         "ctx",
     )
-    back_linear = lax.all_gather(back_part, "tp", axis=1, tiled=True)
+    back_linear = match_scales_in("tp", back_part)
     columns = back_linear
     grad_w1 = (
         lax.psum_scatter(row_product(columns, normed), "ctx", scatter_dimension=0, tiled=True)

time: 357 us -> 408 us (1.14)
  waiting for transfers between devices: 216 us -> 259 us
  starting transfers between devices: 4.98 us -> 10.1 us
  local copies, waits for them, and re-layouts: 15.2 us -> 19.7 us
    all_to_all x0 -> x1, waiting for transfers between devices: none -> 114 us  [match_scales_in(): jax.lax.all_to_all(w2, axis_name=named_axis, split_axis=0, concat_axis=0)]
    all_gather x1 -> x0, waiting for transfers between devices: 69.9 us -> none  [per_device(): back_linear = lax.all_gather(back_part, 'tp', axis=1, tiled=True)]
    all_to_all x0 -> x1, starting transfers between devices: none -> 5.12 us  [match_scales_in(): jax.lax.all_to_all(w2, axis_name=named_axis, split_axis=0, concat_axis=0)]
    another operation x0 -> x1, local copies, waits for them, and re-layouts: none -> 4.3 us  [match_scales_in(): jnp.stack([piece_in for _ in range(jax.lax.psum(1, axis_name=named_axis))...]
  transfers between devices with their start and end apart: 5 -> 5, of which waited for: 3 -> 3; matrix products, arithmetic and copies ran while one was open for 17% -> 15% of each run, Pallas kernels for 0% -> 0%
where the time goes in v1:
time: 408 us; the launch traced here: 407 us
  waiting for transfers between devices  259 us (63%)
  blocking collectives  49.4 us (12%)
  matrix products  40.1 us (10%)
  local copies, waits for them, and re-layouts  19.7 us (5%)
  other arithmetic  15 us (4%)
  between operations  13.9 us (3%)
  starting transfers between devices  10.1 us (2%)
    all_to_all x1, waiting for transfers between devices, match_scales_in(): jax.lax.all_to_all(w2, axis_name=named_axis, split_axis=0, concat_axis=0)  114 us
    all_gather x1, waiting for transfers between devices, per_device(): full_grad = lax.all_gather(out_grad, 'tp', axis=1, tiled=True)  83.1 us
    all_to_all x1, waiting for transfers between devices, per_device(): lax.all_to_all(outgoing, 'tp', split_axis=0, concat_axis=1, tiled=True)  61.1 us
    psum x1, blocking collectives, per_device(): lax.psum((jnp.sum(gained, axis=-1), jnp.sum(gained * features, axis=-1)),...  38.6 us
    dot_general x2, matrix products, row_product(): lax.dot_general(left, right, (((0,), (0,)), ((), ())), preferred_element_...  21 us
    dot_general x1, matrix products, per_device(): norm_grad = jnp.dot(back_linear, w_up, preferred_element_type=jnp.float32)  13 us
    unnamed x18, local copies, waits for them, and re-layouts  11.3 us
    psum x1, blocking collectives, per_device(): lax.psum((jnp.sum(out_grad.astype(jnp.float32), axis=0), jnp.sum(back_par...  10.9 us
  transfers between devices with their start and end apart: 5, of which 3 were waited for; matrix products, arithmetic and copies ran while one was open for 15% of the time, Pallas kernels for 0%

profile of v1, /device:TPU:6, one launch (start us, length us, event | category | flops | bytes accessed | tf_op | source)
XLA Modules:
  0.0 407.4 jit_solution(8701531166109159338)
XLA Ops:
  7.2 0.0 all-gather.2.cloned.1.call-start
  7.2 0.7 all-gather.2.cloned.1.call-update
  7.9 83.1 %all-gather.2.cloned.1.call-done = bf16[1024,4096]{1,0:T(8,128)(2,1)} async-done(((bf16[1024,256]{1,0:T(8,128)(2,1)}), bf16[1024,4096]{1,0:T(8,128)(2,1)}) %all-gather.2.cloned.1.call-update) | async-done | bytes 8388624 | tf_op jit(solution)/shard_map/all_gather | solution.py:40
  91.0 6.0 %convert_reduce_fusion.1 = (f32[256]{0:T(256)S(1)}, bf16[1024,256]{1,0:T(8,128)(2,1)S(1)}) fusion(bf16[1024,256]{1,0:T(8,128)(2,1)} %param.9, bf16[1024,4096]{1,0:T(8,128)(2,1)} %all-gather.2.cloned.1.call-done, bf16[4096,256]{1,0:T(8,128)(2,1)S(1)} %copy-done), kind=kOutput, calls=%fused_computation.28 | convolution fusion | flops 2150891264 | bytes 11535360 | tf_op jit(solution)/shard_map/dot_general | solution.py:41
  97.0 0.2 copy.20
  97.2 4.3 %stack.8 = bf16[16,1024,256]{1,2,0:T(8,128)(2,1)} broadcast(bf16[1024,256]{0,1:T(8,128)(2,1)S(1)} %copy.20), dimensions={1,2} | broadcast | bytes 8912896 | tf_op jit(solution)/shard_map/stack | solution.py:29
  101.5 5.1 %all-to-all-start = ((bf16[16,1024,256]{1,2,0:T(8,128)(2,1)}), bf16[16,1024,256]{1,2,0:T(8,128)(2,1)}, u32[]{:S(2)}, u32[]{:S(2)}) async-start(bf16[16,1024,256]{1,2,0:T(8,128)(2,1)} %stack.8), calls=%async_computation.1 | async-start | bytes 16777216 | tf_op jit(solution)/shard_map/all_to_all | solution.py:30
  106.6 0.0 reduce-scatter.3.cloned.1.call-start
  106.7 7.8 %convolution_bitcast_fusion = f32[4096,256]{0,1:T(8,128)} fusion(bf16[1024,4096]{1,0:T(8,128)(2,1)} %all-gather.2.cloned.1.call-done, bf16[1024,256]{1,0:T(8,128)(2,1)S(1)} %copy-done.4), kind=kOutput, calls=%fused_computation.2 | convolution fusion | flops 2149056512 | bytes 13107200 | tf_op jit(solution)/shard_map/dot_general | solution.py:21
  114.5 0.0 reduce-scatter.5.cloned.1.call-start
  114.6 114.3 %all-to-all-done = bf16[16,1024,256]{1,2,0:T(8,128)(2,1)} async-done(((bf16[16,1024,256]{1,2,0:T(8,128)(2,1)}), bf16[16,1024,256]{1,2,0:T(8,128)(2,1)}, u32[]{:S(2)}, u32[]{:S(2)}) %all-to-all-start) | async-done | bytes 8388640 | tf_op jit(solution)/shard_map/all_to_all | solution.py:30
  228.8 13.3 %fusion.19 = f32[4096,800]{0,1:T(8,128)} fusion(bf16[1024,4096]{0,1:T(8,128)(2,1)} %bitcast.2, bf16[1024,800]{0,1:T(8,128)(2,1)S(1)} %copy-done.3), kind=kOutput, calls=%fused_computation.49 | convolution fusion | flops 6710886400 | bytes 23134208 | tf_op jit(solution)/shard_map/dot_general | solution.py:21
  242.1 0.6 copy-done.7
  242.7 0.2 convert_reduce_fusion.2
  242.9 0.1 select_reduce_fusion
  243.0 0.1 fusion.14
  243.1 13.0 %fusion.1 = (f32[1024]{0:T(1024)S(1)}, f32[800]{0:T(1024)S(1)}, f32[1024]{0:T(1024)S(1)}, f32[800]{0:T(1024)S(1)}, f32[1024,800]{0,1:T(8,128)}) fusion(bf16[1024,800]{0,1:T(8,128)(2,1)S(1)} %copy-done.3, f32[800]{0:T(1024)S(1)} %copy-done.5, bf16[4096,800]{0,1:T(8,128)(2,1)} %param.12, bf16[1024,4096]{0,1:T(8,128)(2,1)} %bitcast.2), kind=kOutput, calls=%fused_computation.7 | convolution fusion | flops 6717435904 | bytes 19875200 | tf_op jit(solution)/shard_map/dot_general | solution.py:61
  256.2 38.6 %all-reduce = (f32[1024]{0:T(1024)S(1)}, f32[1024]{0:T(1024)S(1)}) all-reduce(f32[1024]{0:T(1024)S(1)} %get-tuple-element.24, f32[1024]{0:T(1024)S(1)} %get-tuple-element.26), channel_id=1, replica_groups=mesh['ctx'=8,'tp'=16] {'tp'}, use_global_device_ids=true, to_apply=%region_16.17 | all-reduce | flops 2048 | bytes 16384 | tf_op jit(solution)/shard_map/psum | solution.py:64
  294.8 2.8 fusion.4
  297.6 0.1 copy.26
  297.7 3.8 gather_fusion
  301.4 6.6 %select_select_fusion = bf16[16,256,800]{1,2,0:T(8,128)(2,1)} fusion(bf16[16,256,800]{1,2,0:T(8,128)(2,1)} %gather_fusion, pred[16]{0:T(512)(128)(4,1)S(1)} %compare_and_fusion, pred[16]{0:T(512)(128)(4,1)S(1)} %fusion.14), kind=kLoop, calls=%fused_computation.1 | loop fusion | flops 6553600 | bytes 13107232 | tf_op jit(solution)/shard_map/jit(_where)/select_n | solution.py:88
  308.0 4.8 %all-to-all-start.1 = ((bf16[16,256,800]{1,2,0:T(8,128)(2,1)}), bf16[16,256,800]{1,2,0:T(8,128)(2,1)}, u32[]{:S(2)}, u32[]{:S(2)}) async-start(bf16[16,256,800]{1,2,0:T(8,128)(2,1)} %select_select_fusion), calls=%async_computation.3 | async-start | bytes 13107200 | tf_op jit(solution)/shard_map/all_to_all | solution.py:91
  312.9 0.2 convert_reduce_fusion
  313.1 10.9 %all-reduce.1 = (f32[256]{0:T(256)S(1)}, f32[256]{0:T(256)S(1)}, f32[1,800]{1,0:T(1,128)S(1)}, f32[1,800]{1,0:T(1,128)S(1)}) all-reduce(f32[256]{0:T(256)S(1)} %get-tuple-element.34, f32[256]{0:T(256)S(1)} %convert_reduce_fusion, f32[1,800]{1,0:T(1,128)S(1)} %stack.10, f32[1,800]{1,0:T(1,128)S(1)} %stack.9), channel_id=1, replica_groups=mesh['ctx'=8,'tp'=16] {'ctx'}, use_global_device_ids=true, to_apply=%region_3.0 | all-reduce | flops 2112 | bytes 16896 | tf_op jit(solution)/shard_map/psum | solution.py:48
  323.9 0.6 maximum_multiply_fusion
  324.6 0.6 broadcast_multiply_fusion.4
  325.1 1.1 broadcast_multiply_fusion.1
  326.2 1.0 copy.22
  327.2 61.1 %all-to-all-done.1 = bf16[16,256,800]{1,2,0:T(8,128)(2,1)} async-done(((bf16[16,256,800]{1,2,0:T(8,128)(2,1)}), bf16[16,256,800]{1,2,0:T(8,128)(2,1)}, u32[]{:S(2)}, u32[]{:S(2)}) %all-to-all-start.1) | async-done | bytes 6553632 | tf_op jit(solution)/shard_map/all_to_all | solution.py:91
  388.4 9.7 %copy.23 = bf16[256,12800]{1,0:T(8,128)(2,1)} copy(bf16[256,12800]{0,1:T(8,128)(2,1)} %bitcast.10) | data formatting | bytes 13107200
  398.1 2.8 broadcast_multiply_fusion
  (26 shorter events, 0.1 us)
Async XLA Ops:
  7.2 83.8 %copy-start = (bf16[4096,256]{1,0:T(8,128)(2,1)S(1)}, bf16[4096,256]{1,0:T(8,128)(2,1)}, u32[]{:S(2)}) copy-start(bf16[4096,256]{1,0:T(8,128)(2,1)} %param.13) | copy-start | bytes 6291460
  7.2 83.8 %all-gather.2.cloned.1.call-start = ((), (), s32[]{:S(2)}) async-start(), calls=%async_computation.4 | async-start | bytes 8912896 | tf_op jit(solution)/shard_map/all_gather | solution.py:40
  101.5 5.2 %copy-start.4 = (bf16[1024,256]{1,0:T(8,128)(2,1)S(1)}, bf16[1024,256]{1,0:T(8,128)(2,1)}, u32[]{:S(2)}) copy-start(bf16[1024,256]{1,0:T(8,128)(2,1)} %param.9) | copy-start | bytes 1572868
  101.5 127.3 %all-to-all-start = ((bf16[16,1024,256]{1,2,0:T(8,128)(2,1)}), bf16[16,1024,256]{1,2,0:T(8,128)(2,1)}, u32[]{:S(2)}, u32[]{:S(2)}) async-start(bf16[16,1024,256]{1,2,0:T(8,128)(2,1)} %stack.8), calls=%async_computation.1 | async-start | bytes 16777216 | tf_op jit(solution)/shard_map/all_to_all | solution.py:30
  106.6 218.5 %reduce-scatter.3.cloned.1.call-start = ((), (), s32[]{:S(2)}) async-start(), calls=%async_computation.5 | async-start | bytes 4718592 | tf_op jit(solution)/shard_map/reduce_scatter | solution.py:45
  114.5 114.3 %copy-start.3 = (bf16[1024,800]{0,1:T(8,128)(2,1)S(1)}, bf16[1024,800]{0,1:T(8,128)(2,1)}, u32[]{:S(2)}) copy-start(bf16[1024,800]{0,1:T(8,128)(2,1)} %param.10) | copy-start | bytes 4915204
  114.5 283.5 %reduce-scatter.5.cloned.1.call-start = ((), (), s32[]{:S(2)}) async-start(), calls=%async_computation.6 | async-start | bytes 14745600 | tf_op jit(solution)/shard_map/reduce_scatter | solution.py:58
  242.1 0.7 copy-start.7
  242.1 1.0 copy-start.5
  243.1 51.6 %copy-start.6 = (f32[1024]{0:T(1024)S(1)}, f32[1024]{0:T(1024)}, u32[]{:S(2)}) copy-start(f32[1024]{0:T(1024)} %param.11) | copy-start | bytes 12292
  308.0 4.9 %copy-start.2 = (bf16[1024,256]{1,0:T(8,128)(2,1)S(1)}, bf16[1024,256]{1,0:T(8,128)(2,1)}, u32[]{:S(2)}) copy-start(bf16[1024,256]{1,0:T(8,128)(2,1)} %param.8) | copy-start | bytes 1572868
  308.0 80.3 %all-to-all-start.1 = ((bf16[16,256,800]{1,2,0:T(8,128)(2,1)}), bf16[16,256,800]{1,2,0:T(8,128)(2,1)}, u32[]{:S(2)}, u32[]{:S(2)}) async-start(bf16[16,256,800]{1,2,0:T(8,128)(2,1)} %select_select_fusion), calls=%async_computation.3 | async-start | bytes 13107200 | tf_op jit(solution)/shard_map/all_to_all | solution.py:91
  388.4 12.5 %copy-start.1 = (bf16[4096,256]{1,0:T(8,128)(2,1)S(1)}, bf16[4096,256]{1,0:T(8,128)(2,1)}, u32[]{:S(2)}) copy-start(bf16[4096,256]{1,0:T(8,128)(2,1)} %param.13) | copy-start | bytes 6291460
Sparse Core Ops, SparseCore 0:
  10.1 80.8 all-gather.1
  114.6 36.5 reduce-scatter.2
  242.2 72.8 reduce-scatter.4
